TPU v7x, 32 devices: a whole 2x2x4 slice. The times are simulated.
32 devices in a mesh: trial: 8 (over z, core), slab: 2 (over y), freq: 2 (over x).
Axes of the slice: x: 2, y: 2, z: 4, core: 2. Of those that a mesh axis runs over, the one named last changes fastest.
Arguments:
- orbitals: float32 [8, 8, 64, 128], P('trial', 'slab'), may hold values from -6 to 6
- energies: float32 [8], P('trial'), may hold values from 0 to 1
- potential: float32 [8, 64, 128], P('slab'), may hold values from 0 to 1
- trials: float32 [64, 8, 64, 128], P('trial', 'slab'), may hold values from -6 to 6
- cheb: float32 [2, 4], P('freq'), may hold values from 0.3 to 1
- shifts: float32 [2], P('freq'), may hold values from -0.5 to 0.5
- column_order: int32 [64], replicated, may hold values from 0 to 63, each once
Outputs:
- gram: float32 [64, 64], P(('trial', 'slab'))
Inputs may be any that keep to these rules, and one draw needn't show every extreme that they name: `column_order`: each of 0 to 63 appears once.
All inputs are finite; a program needn't handle non-finite values.
Results may differ from a plain program's by a relative error of at most 0.00024.
Values sent between devices are 32-bit elements; how exact they have to be, the bound alone decides.
A program may use at most 64 MiB of HBM per device.

v0:
```python
import jax
import jax.numpy as jnp
from jax import lax
from jax.sharding import PartitionSpec as P

KSTEPS = 3


def extended(block, sides, width):
    for axis, dim in sides:
        count = lax.axis_size(axis)
        forward = [(i, i + 1) for i in range(count - 1)]
        backward = [(target, source) for source, target in forward]
        low = lax.ppermute(
            lax.slice_in_dim(block, block.shape[dim] - width, None, axis=dim), axis, forward
        )
        high = lax.ppermute(lax.slice_in_dim(block, 0, width, axis=dim), axis, backward)
        block = jnp.concatenate([low, block, high], axis=dim)
    return block


def lateral(field):
    padded = jnp.pad(field, ((0, 0), (0, 0), (1, 1), (1, 1)))
    total = padded[:, :, 2:, 1:-1] + padded[:, :, :-2, 1:-1]
    return total + padded[:, :, 1:-1, 2:] + padded[:, :, 1:-1, :-2]


def expand(start, operate, coeffs):
    before = start
    now = operate(start)
    response = coeffs[0] * start + coeffs[1] * now
    for order in range(2, KSTEPS + 1):
        after = 2.0 * operate(now) - before
        response = response + coeffs[order] * after
        before, now = (now, after)
    return response


def local(orbitals, energies, potential, trials, cheb, shifts, column_order):
    orb_all, energy_all = (
        lax.all_gather(orbitals, "trial", axis=0, tiled=True),
        lax.all_gather(energies, "trial", axis=0, tiled=True),
    )
    norb = orb_all.shape[0]
    planes = trials.shape[1]
    coeffs = cheb[0]
    shift = shifts[0]
    empty = jnp.zeros(trials.shape, jnp.float32)
    stacked = jnp.concatenate([orb_all, trials, potential[None]], axis=0)
    wide = extended(stacked, (("slab", 1),), KSTEPS)
    orb_wide = wide[:norb]
    trial_wide = wide[norb : norb + trials.shape[0]]
    pot_wide = wide[norb + trials.shape[0]]
    width = wide.shape[1]
    global_plane = lax.axis_index("slab") * planes - KSTEPS + jnp.arange(width, dtype=jnp.int32)
    inside = (global_plane >= 0) & (global_plane < planes * lax.axis_size("slab"))
    keep = inside.astype(jnp.float32)[:, None, None]

    def per_orbital(total, item):
        orbital, energy = item
        coef = pot_wide - energy - shift

        def operate(field):
            padded = jnp.pad(field, ((0, 0), (1, 1), (0, 0), (0, 0)))
            beside = padded[:, 2:] + padded[:, :-2] + lateral(field)
            return (coef[None] * field - 0.5 * beside) / 4.5 * keep[None]

        start = orbital[None] * trial_wide
        response = expand(start, operate, coeffs)[:, KSTEPS : KSTEPS + planes]
        return (total + orbital[None, KSTEPS : KSTEPS + planes] * response, None)

    density, _ = lax.scan(per_orbital, empty, (orb_wide, energy_all))
    spread_rho, spread_trial = (
        lax.all_to_all(density, "trial", split_axis=2, concat_axis=0, tiled=True),
        lax.all_to_all(trials, "trial", split_axis=2, concat_axis=0, tiled=True),
    )
    total_trials = spread_rho.shape[0]
    rho_flat = spread_rho.reshape(total_trials, -1)
    trial_flat = spread_trial.reshape(total_trials, -1)
    columns = jnp.arange(total_trials, dtype=jnp.int32)
    order_table = (column_order[:, None] == columns[None]).astype(jnp.float32)
    rho_sorted = jnp.dot(
        order_table, rho_flat, precision=lax.Precision.HIGHEST, preferred_element_type=jnp.float32
    )
    cells = planes * lax.axis_size("slab") * trials.shape[2] * trials.shape[3]
    factor = 1.0 / jnp.sqrt(jnp.float32(cells * norb))
    picker = (column_order[:, None] == columns[None]).astype(jnp.float32)
    left = jnp.dot(
        picker, trial_flat, precision=lax.Precision.HIGHEST, preferred_element_type=jnp.float32
    )
    product = jnp.dot(
        left, rho_sorted.T, precision=lax.Precision.HIGHEST, preferred_element_type=jnp.float32
    )
    partial_rows = lax.psum_scatter(
        product * factor, ("trial", "slab"), scatter_dimension=0, tiled=True
    )
    return lax.psum(partial_rows, "freq")


def solution(mesh):
    in_specs = (
        P("trial", "slab", None, None),
        P("trial"),
        P("slab", None, None),
        P("trial", "slab", None, None),
        P("freq", None),
        P("freq"),
        P(),
    )
    out_specs = P(("trial", "slab"), None)
    return jax.shard_map(local, mesh=mesh, in_specs=in_specs, out_specs=out_specs, check_vma=False)
```

profile of v0, /device:TPU:0, one launch (start us, length us, event | category | flops | bytes accessed | tf_op | source)
XLA Modules:
  0.0 376.7 jit_solution(11273846128169070083)
XLA Ops:
  7.3 26.7 %all-gather.2.cloned.1.call-done = f32[8,4,64,128]{3,2,1,0:T(8,128)} async-done(((f32[1,4,64,128]{3,2,1,0:T(8,128)}), f32[8,4,64,128]{3,2,1,0:T(8,128)}) %all-gather.2.cloned.1.call-update) | async-done | bytes 1048592 | tf_op jit(solution)/shard_map/all_gather | solution.py:41
  37.8 4.8 %collective-permute-start = (f32[17,3,64,128]{3,2,1,0:T(8,128)}, f32[17,3,64,128]{3,2,1,0:T(8,128)}, u32[]{:S(2)}, u32[]{:S(2)}) collective-permute-start(f32[17,3,64,128]{3,2,1,0:T(8,128)} %get-tuple-element.178), channel_id=1, source_target_pairs={{0,2},{1,3},{4,6},{5,7},{8,10},{9,11},{12,14},{13,15},{16,18},{17,... | collective-permute-start | bytes 5013512 | tf_op jit(solution)/shard_map/ppermute | solution.py:14
  47.5 4.2 %all-to-all-start = ((f32[8,4,64,128]{3,0,1,2:T(8,128)}), f32[8,4,64,128]{3,0,1,2:T(8,128)}, u32[]{:S(2)}, u32[]{:S(2)}) async-start(f32[8,4,64,128]{3,0,1,2:T(8,128)} %copy.14), calls=%async_computation | async-start | bytes 2097152 | tf_op jit(solution)/shard_map/all_to_all | solution.py:75
  51.8 29.3 %all-reduce.6 = f32[8]{0:T(128)S(1)} all-reduce(f32[8]{0:T(128)S(1)} %dynamic-update-slice), channel_id=1, replica_groups=mesh['trial'=8,'slab'=2,'freq'=2] {'trial'}, use_global_device_ids=true, to_apply=%add.6 | all-reduce | flops 8 | bytes 64
  85.4 3.0 fusion.41
  89.4 175.6 %while.13 = (s32[]{:T(128)}, f32[8,4,64,128]{3,2,1,0:T(8,128)}, f32[8,10,64,128]{3,2,1,0:T(8,128)}, f32[4]{0:T(128)S(1)}, f32[8,10,64,128]{3,2,1,0:T(8,128)}, /*...) while((s32[]{:T(128)}, f32[8,4,64,128]{3,2,1,0:T(8,128)}, ...), condition=%wide.region_1.2_spmd.clone, body=%wide.region_0.1_spmd.clone.sunk | while | flops 22839348 | bytes 68026840 | solution.py:72
  96.3 3.8 %broadcast_multiply_fusion.5 = (f32[8,10,64,128]{3,2,1,0:T(8,128)}, f32[8,10,64,128]{3,2,1,0:T(8,128)S(1)}) fusion(f32[10,64,128]{2,1,0:T(8,128)S(1)} %subtract_subtract_fusion.2, f32[10]{0:T(128)S(1)} %and_select_fusion.2, f32[8,10,64,128]{3,2,1,0:T(8,128)S(1)} %fusion.51, f32[8,10,64,128]{3,2,1,0:T(8,128)S(1)} %copy-done.2, ...), kind=kLoop, calls=%fused_computation.43.clone.1 | loop fusion | flops 8519680 | bytes 11141160 | tf_op jit(solution)/shard_map/while/body/eval_jaxpr/mul | solution.py:66
  100.1 2.9 fusion.52
  104.7 6.4 %fusion.54 = f32[8,4,64,128]{3,2,1,0:T(8,128)} fusion(f32[8,10,64,128]{3,2,1,0:T(8,128)} %copy-done.1, f32[8,10,64,128]{3,2,1,0:T(8,128)S(1)} %broadcast_multiply_fusion.4, f32[8,10,64,128]{3,2,1,0:T(8,128)} %fusion.52, f32[8,10,64,128]{3,2,1,0:T(8,128)} %get-tuple-element.242, f32[8,4,64,128]{3,2,1,0:T(8,128)} %get-tuple-element.260, ...), kind=kLoop, calls=%fused_computation.49.clone.1 | loop fusion | flops 3670016 | bytes 7471137 | tf_op jit(solution)/shard_map/while/body/eval_jaxpr/add | solution.py:70
  118.0 3.8 %broadcast_multiply_fusion.5 = (f32[8,10,64,128]{3,2,1,0:T(8,128)}, f32[8,10,64,128]{3,2,1,0:T(8,128)S(1)}) fusion(f32[10,64,128]{2,1,0:T(8,128)S(1)} %subtract_subtract_fusion.2, f32[10]{0:T(128)S(1)} %and_select_fusion.2, f32[8,10,64,128]{3,2,1,0:T(8,128)S(1)} %fusion.51, f32[8,10,64,128]{3,2,1,0:T(8,128)S(1)} %copy-done.2, ...), kind=kLoop, calls=%fused_computation.43.clone.1 | loop fusion | flops 8519680 | bytes 11141160 | tf_op jit(solution)/shard_map/while/body/eval_jaxpr/mul | solution.py:66
  121.8 2.9 fusion.52
  126.4 6.7 %fusion.54 = f32[8,4,64,128]{3,2,1,0:T(8,128)} fusion(f32[8,10,64,128]{3,2,1,0:T(8,128)} %copy-done.1, f32[8,10,64,128]{3,2,1,0:T(8,128)S(1)} %broadcast_multiply_fusion.4, f32[8,10,64,128]{3,2,1,0:T(8,128)} %fusion.52, f32[8,10,64,128]{3,2,1,0:T(8,128)} %get-tuple-element.242, f32[8,4,64,128]{3,2,1,0:T(8,128)} %get-tuple-element.260, ...), kind=kLoop, calls=%fused_computation.49.clone.1 | loop fusion | flops 3670016 | bytes 7471137 | tf_op jit(solution)/shard_map/while/body/eval_jaxpr/add | solution.py:70
  140.0 3.8 %broadcast_multiply_fusion.5 = (f32[8,10,64,128]{3,2,1,0:T(8,128)}, f32[8,10,64,128]{3,2,1,0:T(8,128)S(1)}) fusion(f32[10,64,128]{2,1,0:T(8,128)S(1)} %subtract_subtract_fusion.2, f32[10]{0:T(128)S(1)} %and_select_fusion.2, f32[8,10,64,128]{3,2,1,0:T(8,128)S(1)} %fusion.51, f32[8,10,64,128]{3,2,1,0:T(8,128)S(1)} %copy-done.2, ...), kind=kLoop, calls=%fused_computation.43.clone.1 | loop fusion | flops 8519680 | bytes 11141160 | tf_op jit(solution)/shard_map/while/body/eval_jaxpr/mul | solution.py:66
  143.8 2.9 fusion.52
  148.3 6.7 %fusion.54 = f32[8,4,64,128]{3,2,1,0:T(8,128)} fusion(f32[8,10,64,128]{3,2,1,0:T(8,128)} %copy-done.1, f32[8,10,64,128]{3,2,1,0:T(8,128)S(1)} %broadcast_multiply_fusion.4, f32[8,10,64,128]{3,2,1,0:T(8,128)} %fusion.52, f32[8,10,64,128]{3,2,1,0:T(8,128)} %get-tuple-element.242, f32[8,4,64,128]{3,2,1,0:T(8,128)} %get-tuple-element.260, ...), kind=kLoop, calls=%fused_computation.49.clone.1 | loop fusion | flops 3670016 | bytes 7471137 | tf_op jit(solution)/shard_map/while/body/eval_jaxpr/add | solution.py:70
  162.0 3.8 %broadcast_multiply_fusion.5 = (f32[8,10,64,128]{3,2,1,0:T(8,128)}, f32[8,10,64,128]{3,2,1,0:T(8,128)S(1)}) fusion(f32[10,64,128]{2,1,0:T(8,128)S(1)} %subtract_subtract_fusion.2, f32[10]{0:T(128)S(1)} %and_select_fusion.2, f32[8,10,64,128]{3,2,1,0:T(8,128)S(1)} %fusion.51, f32[8,10,64,128]{3,2,1,0:T(8,128)S(1)} %copy-done.2, ...), kind=kLoop, calls=%fused_computation.43.clone.1 | loop fusion | flops 8519680 | bytes 11141160 | tf_op jit(solution)/shard_map/while/body/eval_jaxpr/mul | solution.py:66
  165.8 2.9 fusion.52
  170.3 6.7 %fusion.54 = f32[8,4,64,128]{3,2,1,0:T(8,128)} fusion(f32[8,10,64,128]{3,2,1,0:T(8,128)} %copy-done.1, f32[8,10,64,128]{3,2,1,0:T(8,128)S(1)} %broadcast_multiply_fusion.4, f32[8,10,64,128]{3,2,1,0:T(8,128)} %fusion.52, f32[8,10,64,128]{3,2,1,0:T(8,128)} %get-tuple-element.242, f32[8,4,64,128]{3,2,1,0:T(8,128)} %get-tuple-element.260, ...), kind=kLoop, calls=%fused_computation.49.clone.1 | loop fusion | flops 3670016 | bytes 7471137 | tf_op jit(solution)/shard_map/while/body/eval_jaxpr/add | solution.py:70
  184.0 3.8 %broadcast_multiply_fusion.5 = (f32[8,10,64,128]{3,2,1,0:T(8,128)}, f32[8,10,64,128]{3,2,1,0:T(8,128)S(1)}) fusion(f32[10,64,128]{2,1,0:T(8,128)S(1)} %subtract_subtract_fusion.2, f32[10]{0:T(128)S(1)} %and_select_fusion.2, f32[8,10,64,128]{3,2,1,0:T(8,128)S(1)} %fusion.51, f32[8,10,64,128]{3,2,1,0:T(8,128)S(1)} %copy-done.2, ...), kind=kLoop, calls=%fused_computation.43.clone.1 | loop fusion | flops 8519680 | bytes 11141160 | tf_op jit(solution)/shard_map/while/body/eval_jaxpr/mul | solution.py:66
  187.7 2.9 fusion.52
  192.3 6.7 %fusion.54 = f32[8,4,64,128]{3,2,1,0:T(8,128)} fusion(f32[8,10,64,128]{3,2,1,0:T(8,128)} %copy-done.1, f32[8,10,64,128]{3,2,1,0:T(8,128)S(1)} %broadcast_multiply_fusion.4, f32[8,10,64,128]{3,2,1,0:T(8,128)} %fusion.52, f32[8,10,64,128]{3,2,1,0:T(8,128)} %get-tuple-element.242, f32[8,4,64,128]{3,2,1,0:T(8,128)} %get-tuple-element.260, ...), kind=kLoop, calls=%fused_computation.49.clone.1 | loop fusion | flops 3670016 | bytes 7471137 | tf_op jit(solution)/shard_map/while/body/eval_jaxpr/add | solution.py:70
  205.9 3.8 %broadcast_multiply_fusion.5 = (f32[8,10,64,128]{3,2,1,0:T(8,128)}, f32[8,10,64,128]{3,2,1,0:T(8,128)S(1)}) fusion(f32[10,64,128]{2,1,0:T(8,128)S(1)} %subtract_subtract_fusion.2, f32[10]{0:T(128)S(1)} %and_select_fusion.2, f32[8,10,64,128]{3,2,1,0:T(8,128)S(1)} %fusion.51, f32[8,10,64,128]{3,2,1,0:T(8,128)S(1)} %copy-done.2, ...), kind=kLoop, calls=%fused_computation.43.clone.1 | loop fusion | flops 8519680 | bytes 11141160 | tf_op jit(solution)/shard_map/while/body/eval_jaxpr/mul | solution.py:66
  214.3 6.7 %fusion.54 = f32[8,4,64,128]{3,2,1,0:T(8,128)} fusion(f32[8,10,64,128]{3,2,1,0:T(8,128)} %copy-done.1, f32[8,10,64,128]{3,2,1,0:T(8,128)S(1)} %broadcast_multiply_fusion.4, f32[8,10,64,128]{3,2,1,0:T(8,128)} %fusion.52, f32[8,10,64,128]{3,2,1,0:T(8,128)} %get-tuple-element.242, f32[8,4,64,128]{3,2,1,0:T(8,128)} %get-tuple-element.260, ...), kind=kLoop, calls=%fused_computation.49.clone.1 | loop fusion | flops 3670016 | bytes 7471137 | tf_op jit(solution)/shard_map/while/body/eval_jaxpr/add | solution.py:70
  227.9 3.8 %broadcast_multiply_fusion.5 = (f32[8,10,64,128]{3,2,1,0:T(8,128)}, f32[8,10,64,128]{3,2,1,0:T(8,128)S(1)}) fusion(f32[10,64,128]{2,1,0:T(8,128)S(1)} %subtract_subtract_fusion.2, f32[10]{0:T(128)S(1)} %and_select_fusion.2, f32[8,10,64,128]{3,2,1,0:T(8,128)S(1)} %fusion.51, f32[8,10,64,128]{3,2,1,0:T(8,128)S(1)} %copy-done.2, ...), kind=kLoop, calls=%fused_computation.43.clone.1 | loop fusion | flops 8519680 | bytes 11141160 | tf_op jit(solution)/shard_map/while/body/eval_jaxpr/mul | solution.py:66
  236.3 6.7 %fusion.54 = f32[8,4,64,128]{3,2,1,0:T(8,128)} fusion(f32[8,10,64,128]{3,2,1,0:T(8,128)} %copy-done.1, f32[8,10,64,128]{3,2,1,0:T(8,128)S(1)} %broadcast_multiply_fusion.4, f32[8,10,64,128]{3,2,1,0:T(8,128)} %fusion.52, f32[8,10,64,128]{3,2,1,0:T(8,128)} %get-tuple-element.242, f32[8,4,64,128]{3,2,1,0:T(8,128)} %get-tuple-element.260, ...), kind=kLoop, calls=%fused_computation.49.clone.1 | loop fusion | flops 3670016 | bytes 7471137 | tf_op jit(solution)/shard_map/while/body/eval_jaxpr/add | solution.py:70
  249.9 3.8 %broadcast_multiply_fusion.5 = (f32[8,10,64,128]{3,2,1,0:T(8,128)}, f32[8,10,64,128]{3,2,1,0:T(8,128)S(1)}) fusion(f32[10,64,128]{2,1,0:T(8,128)S(1)} %subtract_subtract_fusion.2, f32[10]{0:T(128)S(1)} %and_select_fusion.2, f32[8,10,64,128]{3,2,1,0:T(8,128)S(1)} %fusion.51, f32[8,10,64,128]{3,2,1,0:T(8,128)S(1)} %copy-done.2, ...), kind=kLoop, calls=%fused_computation.43.clone.1 | loop fusion | flops 8519680 | bytes 11141160 | tf_op jit(solution)/shard_map/while/body/eval_jaxpr/mul | solution.py:66
  253.7 2.9 fusion.52
  258.3 6.7 %fusion.54 = f32[8,4,64,128]{3,2,1,0:T(8,128)} fusion(f32[8,10,64,128]{3,2,1,0:T(8,128)} %copy-done.1, f32[8,10,64,128]{3,2,1,0:T(8,128)S(1)} %broadcast_multiply_fusion.4, f32[8,10,64,128]{3,2,1,0:T(8,128)} %fusion.52, f32[8,10,64,128]{3,2,1,0:T(8,128)} %get-tuple-element.242, f32[8,4,64,128]{3,2,1,0:T(8,128)} %get-tuple-element.260, ...), kind=kLoop, calls=%fused_computation.49.clone.1 | loop fusion | flops 3670016 | bytes 7471137 | tf_op jit(solution)/shard_map/while/body/eval_jaxpr/add | solution.py:70
  267.9 4.4 %all-to-all-start.1 = ((f32[8,4,64,128]{3,1,0,2:T(4,128)}), f32[8,4,64,128]{3,1,0,2:T(4,128)S(1)}, u32[]{:S(2)}, u32[]{:S(2)}) async-start(f32[8,4,64,128]{3,1,0,2:T(4,128)} %copy.16), calls=%async_computation.1 | async-start | bytes 2097152 | tf_op jit(solution)/shard_map/all_to_all | solution.py:74
  276.3 22.6 %all-to-all-done.1 = f32[8,4,64,128]{3,1,0,2:T(4,128)S(1)} async-done(((f32[8,4,64,128]{3,1,0,2:T(4,128)}), f32[8,4,64,128]{3,1,0,2:T(4,128)S(1)}, u32[]{:S(2)}, u32[]{:S(2)}) %all-to-all-start.1) | async-done | bytes 1048608 | tf_op jit(solution)/shard_map/all_to_all | solution.py:74
  303.5 60.9 %all-reduce.7 = f32[64,64]{1,0:T(8,128)S(1)} all-reduce(f32[64,64]{1,0:T(8,128)S(1)} %convolution_multiply_fusion), channel_id=2, replica_groups=mesh['trial'=8,'slab'=2,'freq'=2] {'trial','slab'}, use_global_device_ids=true, to_apply=%region_2.3.clone | all-reduce | flops 4096 | bytes 32768
  364.4 5.5 %psum.7 = f32[4,64]{1,0:T(4,128)} all-reduce(f32[4,64]{1,0:T(4,128)S(1)} %constant_dynamic-slice_fusion), channel_id=1, replica_groups=mesh['trial'=8,'slab'=2,'freq'=2] {'freq'}, use_global_device_ids=true, to_apply=%region_3.4 | all-reduce | flops 256 | bytes 2048 | tf_op jit(solution)/shard_map/psum | solution.py:97
  (161 shorter events, 98.9 us)
Async XLA Ops:
  6.5 27.4 %all-gather.2.cloned.1.call-start = ((), (), s32[]{:S(2)}) async-start(), calls=%async_computation.2 | async-start | bytes 1179648 | tf_op jit(solution)/shard_map/all_gather | solution.py:41
  35.7 8.2 %copy-start.3 = (f32[8,4,64,128]{3,2,1,0:T(8,128)S(1)}, f32[8,4,64,128]{3,2,1,0:T(8,128)}, u32[]{:S(2)}) copy-start(f32[8,4,64,128]{3,2,1,0:T(8,128)} %param.12) | copy-start | bytes 3145732
  35.7 10.5 %copy-start.9 = (u32[32]{0:T(128)S(1)}, u32[32]{0:T(128)}, u32[]{:S(2)}) copy-start(u32[32]{0:T(128)} %constant.76) | copy-start | bytes 388
  37.8 45.3 %copy-start.4 = (f32[8,4,64,128]{3,2,1,0:T(8,128)S(1)}, f32[8,4,64,128]{3,2,1,0:T(8,128)}, u32[]{:S(2)}) copy-start(f32[8,4,64,128]{3,2,1,0:T(8,128)} %all-gather.2.cloned.1.call-done) | copy-start | bytes 3145732
  37.8 45.3 %copy-start.5 = (f32[4,64,128]{2,1,0:T(8,128)S(1)}, f32[4,64,128]{2,1,0:T(8,128)}, u32[]{:S(2)}) copy-start(f32[4,64,128]{2,1,0:T(8,128)} %param.11) | copy-start | bytes 393220
  37.8 43.3 %collective-permute-start = (f32[17,3,64,128]{3,2,1,0:T(8,128)}, f32[17,3,64,128]{3,2,1,0:T(8,128)}, u32[]{:S(2)}, u32[]{:S(2)}) collective-permute-start(f32[17,3,64,128]{3,2,1,0:T(8,128)} %get-tuple-element.178), channel_id=1, source_target_pairs={{0,2},{1,3},{4,6},{5,7},{8,10},{9,11},{12,14},{13,15},{16,18},{17,... | collective-permute-start | bytes 5013512 | tf_op jit(solution)/shard_map/ppermute | solution.py:14
  42.6 40.5 %collective-permute-start.1 = (f32[17,3,64,128]{3,2,1,0:T(8,128)}, f32[17,3,64,128]{3,2,1,0:T(8,128)}, u32[]{:S(2)}, u32[]{:S(2)}) collective-permute-start(f32[17,3,64,128]{3,2,1,0:T(8,128)} %get-tuple-element.179), channel_id=1, source_target_pairs={{2,0},{3,1},{6,4},{7,5},{10,8},{11,9},{14,12},{15,13},{18,16},{19,... | collective-permute-start | bytes 5013512 | tf_op jit(solution)/shard_map/ppermute | solution.py:17
  47.5 220.4 %all-to-all-start = ((f32[8,4,64,128]{3,0,1,2:T(8,128)}), f32[8,4,64,128]{3,0,1,2:T(8,128)}, u32[]{:S(2)}, u32[]{:S(2)}) async-start(f32[8,4,64,128]{3,0,1,2:T(8,128)} %copy.14), calls=%async_computation | async-start | bytes 2097152 | tf_op jit(solution)/shard_map/all_to_all | solution.py:75
  94.2 2.1 copy-start.2
  96.3 3.8 %copy-start = (f32[8,10,64,128]{3,2,1,0:T(8,128)}, f32[8,10,64,128]{3,2,1,0:T(8,128)S(1)}, u32[]{:S(2)}) copy-start(f32[8,10,64,128]{3,2,1,0:T(8,128)S(1)} %fusion.51) | copy-start | bytes 7864324 | tf_op jit(solution)/shard_map/while
  100.1 2.9 copy-start.1
  115.9 2.1 copy-start.2
  118.0 3.8 %copy-start = (f32[8,10,64,128]{3,2,1,0:T(8,128)}, f32[8,10,64,128]{3,2,1,0:T(8,128)S(1)}, u32[]{:S(2)}) copy-start(f32[8,10,64,128]{3,2,1,0:T(8,128)S(1)} %fusion.51) | copy-start | bytes 7864324 | tf_op jit(solution)/shard_map/while
  121.8 2.9 copy-start.1
  140.0 3.8 %copy-start = (f32[8,10,64,128]{3,2,1,0:T(8,128)}, f32[8,10,64,128]{3,2,1,0:T(8,128)S(1)}, u32[]{:S(2)}) copy-start(f32[8,10,64,128]{3,2,1,0:T(8,128)S(1)} %fusion.51) | copy-start | bytes 7864324 | tf_op jit(solution)/shard_map/while
  143.8 2.9 copy-start.1
  162.0 3.8 %copy-start = (f32[8,10,64,128]{3,2,1,0:T(8,128)}, f32[8,10,64,128]{3,2,1,0:T(8,128)S(1)}, u32[]{:S(2)}) copy-start(f32[8,10,64,128]{3,2,1,0:T(8,128)S(1)} %fusion.51) | copy-start | bytes 7864324 | tf_op jit(solution)/shard_map/while
  165.8 2.9 copy-start.1
  181.8 2.1 copy-start.2
  183.9 3.8 %copy-start = (f32[8,10,64,128]{3,2,1,0:T(8,128)}, f32[8,10,64,128]{3,2,1,0:T(8,128)S(1)}, u32[]{:S(2)}) copy-start(f32[8,10,64,128]{3,2,1,0:T(8,128)S(1)} %fusion.51) | copy-start | bytes 7864324 | tf_op jit(solution)/shard_map/while
  187.7 2.9 copy-start.1
  203.8 2.1 copy-start.2
  205.9 3.8 %copy-start = (f32[8,10,64,128]{3,2,1,0:T(8,128)}, f32[8,10,64,128]{3,2,1,0:T(8,128)S(1)}, u32[]{:S(2)}) copy-start(f32[8,10,64,128]{3,2,1,0:T(8,128)S(1)} %fusion.51) | copy-start | bytes 7864324 | tf_op jit(solution)/shard_map/while
  209.7 2.9 copy-start.1
  225.8 2.1 copy-start.2
  227.9 3.8 %copy-start = (f32[8,10,64,128]{3,2,1,0:T(8,128)}, f32[8,10,64,128]{3,2,1,0:T(8,128)S(1)}, u32[]{:S(2)}) copy-start(f32[8,10,64,128]{3,2,1,0:T(8,128)S(1)} %fusion.51) | copy-start | bytes 7864324 | tf_op jit(solution)/shard_map/while
  231.7 2.9 copy-start.1
  249.9 3.8 %copy-start = (f32[8,10,64,128]{3,2,1,0:T(8,128)}, f32[8,10,64,128]{3,2,1,0:T(8,128)S(1)}, u32[]{:S(2)}) copy-start(f32[8,10,64,128]{3,2,1,0:T(8,128)S(1)} %fusion.51) | copy-start | bytes 7864324 | tf_op jit(solution)/shard_map/while
  253.7 2.9 copy-start.1
  265.0 7.3 %copy-start.8 = (u32[32]{0:T(128)S(1)}, u32[32]{0:T(128)}, u32[]{:S(2)}) copy-start(u32[32]{0:T(128)} %constant.83) | copy-start | bytes 388
  267.9 31.0 %all-to-all-start.1 = ((f32[8,4,64,128]{3,1,0,2:T(4,128)}), f32[8,4,64,128]{3,1,0,2:T(4,128)S(1)}, u32[]{:S(2)}, u32[]{:S(2)}) async-start(f32[8,4,64,128]{3,1,0,2:T(4,128)} %copy.16), calls=%async_computation.1 | async-start | bytes 2097152 | tf_op jit(solution)/shard_map/all_to_all | solution.py:74
  272.3 3.3 copy-start.7
  (4 other events, 7.3 us)
Sparse Core Ops, SparseCore 0:
  8.9 24.9 all-gather.1
where the time goes:
time: 378 us; the launch traced here: 377 us
  other arithmetic  154 us (41%)
  blocking collectives  95.7 us (25%)
  waiting for transfers between devices  52.1 us (14%)
  local copies, waits for them, and re-layouts  42.3 us (11%)
  between operations  14.9 us (4%)
  starting transfers between devices  14.7 us (4%)
    unnamed x2, blocking collectives  90.2 us
    mul x32, other arithmetic, operate(): return (coef[None] * field - 0.5 * beside) / 4.5 * keep[None]  70.2 us
    add x8, other arithmetic, per_orbital(): return (total + orbital[None, KSTEPS:KSTEPS + planes] * response, None)  53.4 us
    all_gather x1, waiting for transfers between devices, local(): lax.all_gather(orbitals, 'trial', axis=0, tiled=True)  26.7 us
    all_to_all x1, waiting for transfers between devices, local(): lax.all_to_all(density, 'trial', split_axis=2, concat_axis=0, tiled=True)  22.6 us
    mul x8, other arithmetic, per_orbital(): start = orbital[None] * trial_wide  16 us
    sub x8, other arithmetic, per_orbital(): coef = pot_wide - energy - shift  9.73 us
    mul x8, local copies, waits for them, and re-layouts, per_orbital(): start = orbital[None] * trial_wide  7.96 us
  transfers between devices with their start and end apart: 5, of which 3 were waited for; matrix products, arithmetic and copies ran while one was open for 51% of the time, Pallas kernels for 0%

commit v1 on v0

v1 whole, which is shorter than its diff:
```python
import functools

import jax
import jax.numpy as jnp
from jax import lax
from jax.experimental import pallas as pl
from jax.experimental.pallas import tpu as pltpu
from jax.sharding import PartitionSpec as P

REACH = 3
MESH = pl.DeviceIdType.MESH
HIGH = lax.Precision.HIGHEST

OFFSETS = [
    (dx, dy, dz)
    for dz in range(-REACH, REACH + 1)
    for dx in range(REACH + 1)
    for dy in range(-REACH, REACH + 1)
    if abs(dx) + abs(dy) + abs(dz) <= REACH and (dx, dy, dz) >= (0, 0, 0)
]
PATHS = {(1, 1, 1): 6.0, (0, 1, 2): 3.0, (0, 0, 3): 1.0}


def rolled(value, shift):
    shift = shift % value.shape[1]
    return value if shift == 0 else pltpu.roll(value, shift, 1)


def kernel(
    sizes, orb, par, pot, tri, order, out,
    orbs, wide, pots, pars, freqs, scaled, weights, coefs, dens, rho_in, tri_in, rows_out, rows_in,
    near_s, near_r, orb_s, orb_r, pass_s, pass_r, par_s, par_r, frq_s, frq_r,
    tri_s, tri_r, rho_s, rho_r, row_s, row_r, loc,
):
    nt, ns, nf = sizes
    per, planes, ny, nz = tri.shape
    norb = orbs.shape[0]
    half = ny // nf
    window = half + 8
    total = nt * per
    piece = planes * half // nt
    t, s, f = lax.axis_index("trial"), lax.axis_index("slab"), lax.axis_index("freq")
    mate = t + 1 - 2 * lax.rem(t, 2)
    src_y = pl.ds(pl.multiple_of(f * (half - 8), 8), window)
    dst_y = pl.ds(pl.multiple_of(8 - 8 * f, 8), window)
    edge_y = pl.ds(pl.multiple_of(f * window, 8), 8)
    last = s == ns - 1

    orbs[:, :, edge_y, :] = jnp.zeros((norb, planes + REACH, 8, nz), jnp.float32)
    wide[:, :, edge_y, :] = jnp.zeros((per, planes + REACH, 8, nz), jnp.float32)
    pots[:, edge_y, :] = jnp.zeros((planes + REACH + 1, 8, nz), jnp.float32)

    @pl.when(last)
    def _():
        orbs[t, planes:, dst_y, :] = jnp.zeros((REACH, window, nz), jnp.float32)
        wide[:, planes:, dst_y, :] = jnp.zeros((per, REACH, window, nz), jnp.float32)
        pots[planes + 1 :, dst_y, :] = jnp.zeros((REACH, window, nz), jnp.float32)

    @pl.when(s == 0)
    def _():
        pots[0, dst_y, :] = jnp.zeros((window, nz), jnp.float32)

    locals_ = [
        pltpu.make_async_copy(orb.at[0, :, src_y, :], orbs.at[t, :planes, dst_y, :], loc.at[0]),
        pltpu.make_async_copy(tri.at[:, :, src_y, :], wide.at[:, :planes, dst_y, :], loc.at[1]),
        pltpu.make_async_copy(pot.at[:, src_y, :], pots.at[1 : planes + 1, dst_y, :], loc.at[2]),
        pltpu.make_async_copy(par, pars.at[t], loc.at[3]),
        pltpu.make_async_copy(par, freqs.at[f], loc.at[4]),
    ]
    for copy in locals_:
        copy.start()

    def device(k):
        dt, ds, df = k // (ns * nf), (k // nf) % ns, k % nf
        return lax.rem(t + dt, nt), lax.rem(s + ds, ns), lax.rem(f + df, nf)

    count = nt * ns * nf
    barrier = pltpu.get_barrier_semaphore()

    if count <= 64:
        for k in range(1, count):
            pt, ps, pf = device(k)
            pl.semaphore_signal(barrier, inc=1, device_id={"trial": pt, "slab": ps, "freq": pf}, device_id_type=MESH)
    else:

        @pl.loop(1, count)
        def _(k):
            pt, ps, pf = device(k)
            pl.semaphore_signal(barrier, inc=1, device_id={"trial": pt, "slab": ps, "freq": pf}, device_id_type=MESH)

    pl.semaphore_wait(barrier, count - 1)

    def remote(src, dst, send, recv, **where):
        return pltpu.make_async_remote_copy(
            src_ref=src, dst_ref=dst, send_sem=send, recv_sem=recv, device_id=where, device_id_type=MESH
        )

    below, above = jnp.maximum(s - 1, 0), jnp.minimum(s + 1, ns - 1)
    down = [
        remote(orb.at[0, :REACH, src_y, :], orbs.at[t, planes:, dst_y, :], near_s.at[0], near_r.at[0], slab=below),
        remote(tri.at[:, :REACH, src_y, :], wide.at[:, planes:, dst_y, :], near_s.at[1], near_r.at[1], slab=below),
        remote(pot.at[:REACH, src_y, :], pots.at[planes + 1 :, dst_y, :], near_s.at[2], near_r.at[2], slab=below),
    ]
    up = remote(pot.at[planes - 1, src_y, :], pots.at[0, dst_y, :], near_s.at[3], near_r.at[3], slab=above)

    @pl.when(s > 0)
    def _():
        down[0].start()
        down[2].start()
        down[1].start()

    @pl.when(s < ns - 1)
    def _():
        up.start()

    par_copies = []
    for j in range(1, nt):
        par_copies.append(remote(par, pars.at[t], par_s.at[j], par_r.at[j], trial=lax.rem(t + j, nt)))
    for j in range(1, nf):
        par_copies.append(remote(par, freqs.at[f], frq_s.at[j], frq_r.at[j], freq=lax.rem(f + j, nf)))
    for copy in par_copies:
        copy.start()

    for copy in locals_:
        copy.wait()

    @pl.when(s < ns - 1)
    def _():
        down[0].wait_recv()

    def block(slot):
        return orbs.at[slot, :, dst_y, :]

    chips = nt // 2
    orb_copies = []
    for j in range(1, chips):
        orb_copies.append(remote(block(t), block(t), orb_s.at[j], orb_r.at[j], trial=lax.rem(t + 2 * j, nt)))
    pass_copies = [remote(block(t), block(t), pass_s.at[0], pass_r.at[0], trial=mate)]
    for copy in orb_copies + pass_copies:
        copy.start()

    tri_copies = []
    span = half // piece
    for j in range(1, nt):
        peer = lax.rem(t + j, nt)
        y0 = pl.multiple_of(f * half + lax.rem(peer, span) * piece, 8)
        part = tri.at[:, peer // span, pl.ds(y0, piece), :]
        tri_copies.append(remote(part, tri_in.at[t], tri_s.at[j], tri_r.at[j], trial=peer))
    for copy in tri_copies:
        copy.start()
    y0 = pl.multiple_of(f * half + lax.rem(t, span) * piece, 8)
    own_tri = pltpu.make_async_copy(tri.at[:, t // span, pl.ds(y0, piece), :], tri_in.at[t], loc.at[5])
    own_tri.start()

    for j in range(1, chips):
        orb_copies[j - 1].wait_recv()
        source = lax.rem(t - 2 * j + nt, nt)
        copy = remote(block(source), block(source), pass_s.at[j], pass_r.at[j], trial=mate)
        copy.start()
        pass_copies.append(copy)
    for copy in par_copies:
        copy.wait_recv()

    inverse = 1.0 / 4.5
    hop = -0.5 / 4.5
    for i in range(norb):
        energy = pars[i, 0:1, :]
        terms = [0.0, 0.0, 0.0, 0.0]
        for w in range(nf):
            mu = (energy + freqs[w, 5:6, :]) * inverse
            c0, c1, c2, c3 = (freqs[w, 1 + n : 2 + n, :] for n in range(4))
            b0, b1, b2, b3 = c0 - c2, c1 - 3.0 * c3, 2.0 * c2, 4.0 * c3
            terms[0] += b0 - mu * (b1 - mu * (b2 - mu * b3))
            terms[1] += b1 - mu * (2.0 * b2 - 3.0 * mu * b3)
            terms[2] += b2 - 3.0 * mu * b3
            terms[3] += b3
        for n in range(4):
            weights[n, i] = jnp.broadcast_to(terms[n], weights.shape[2:])

    @pl.when(s < ns - 1)
    def _():
        down[1].wait_recv()
        down[2].wait_recv()

    @pl.when(s > 0)
    def _():
        up.wait_recv()

    for copy in pass_copies:
        copy.wait_recv()

    mid = slice(8, 8 + half)
    lane = lax.broadcasted_iota(jnp.int32, (half, nz), 1)
    row = lax.broadcasted_iota(jnp.int32, (half, nz), 0) + f * half

    def links(position, size):
        return (position >= 1).astype(jnp.float32) + (position + 1 < size).astype(jnp.float32)

    def one_plane(x, carry):
        xg = s * planes + x
        column = jnp.zeros((half, nz), jnp.int32) + xg
        for dz in range(-REACH, REACH + 1):
            group = [(n, off) for n, off in enumerate(OFFSETS) if off[2] == dz]
            if not group:
                continue
            depth = lane - dz
            inside = ((depth >= 0) & (depth < nz)).astype(jnp.float32)
            deepest = max(sum(map(abs, off)) for _, off in group)
            least = min(sum(map(abs, off)) for _, off in group)

            def prepare(i, carry):
                centre = rolled(orbs[i, x, mid, :], dz) * inside
                for n in range(least, 4):
                    scaled[n, i] = weights[n, i, 0:1, :] * centre
                return carry

            lax.fori_loop(0, norb, prepare, 0, unroll=True)

            def local(a, b, c):
                return rolled(pots[1 + x + a, 8 + b : 8 + b + half, :], dz - c) * inverse

            for index, (dx, dy, _) in group:
                steps = abs(dx) + abs(dy) + abs(dz)
                sums = {n: 0.0 for n in range(steps, 4)}
                for i in range(norb):
                    there = orbs[i, x + dx, 8 + dy : 8 + dy + half, :]
                    for n in sums:
                        sums[n] = sums[n] + scaled[n, i] * there
                if steps == 3:
                    kind = tuple(sorted(map(abs, (dx, dy, dz))))
                    coef = (PATHS[kind] * hop**3) * sums[3]
                elif steps == 2:
                    here, end = local(0, 0, 0), local(dx, dy, dz)
                    corners = [c for c in ((dx, 0, 0), (0, dy, 0), (0, 0, dz)) if c != (0, 0, 0)]
                    if len(corners) == 1:
                        middle = local(dx // 2, dy // 2, dz // 2)
                        coef = hop**2 * (sums[2] + (here + middle + end) * sums[3])
                    else:
                        middle = local(*corners[0]) + local(*corners[1])
                        coef = hop**2 * (2.0 * sums[2] + (2.0 * (here + end) + middle) * sums[3])
                elif steps == 1:
                    here, end = local(0, 0, 0), local(dx, dy, dz)
                    at = (column, row, depth)
                    size = (planes * ns, ny, nz)
                    move = (dx, dy, dz)
                    side, along = 0.0, 0.0
                    for axis in range(3):
                        if move[axis]:
                            along = links(at[axis], size[axis]) + links(at[axis] + move[axis], size[axis])
                        else:
                            side = side + links(at[axis], size[axis])
                    walks = along + 3.0 * side - 1.0
                    cubic = here * here + here * end + end * end + hop**2 * walks
                    coef = hop * (sums[1] + (here + end) * sums[2] + cubic * sums[3])
                else:
                    here = local(0, 0, 0)
                    degree = links(column, planes * ns) + links(row, ny) + links(lane, nz)
                    near = local(1, 0, 0) + local(-1, 0, 0) + local(0, 1, 0) + local(0, -1, 0)
                    near = near + jnp.where(lane + 1 < nz, local(0, 0, 1), 0.0)
                    near = near + jnp.where(lane >= 1, local(0, 0, -1), 0.0)
                    square = here * here + hop**2 * degree
                    cube = here * (here * here + 2.0 * hop**2 * degree) + hop**2 * near
                    coef = 0.5 * (sums[0] + here * sums[1] + square * sums[2] + cube * sums[3])
                coefs[index] = coef

        def one_trial(k, carry):
            density = 0.0
            for dz in range(-REACH, REACH + 1):
                group = [(n, off) for n, off in enumerate(OFFSETS) if off[2] == dz]
                if not group:
                    continue
                part = 0.0
                for index, (dx, dy, _) in group:
                    part = part + coefs[index] * wide[k, x + dx, 8 + dy : 8 + dy + half, :]
                density = density + rolled(part, -dz)
            for h in range(span):
                dens[x * span + h, k] = density[h * piece : (h + 1) * piece]
            return carry

        return lax.fori_loop(0, per, one_trial, carry)

    lax.fori_loop(0, planes, one_plane, 0)

    rho_copies = []
    for j in range(1, nt):
        peer = lax.rem(t + j, nt)
        rho_copies.append(remote(dens.at[peer], rho_in.at[t], rho_s.at[j], rho_r.at[j], trial=peer))
    for copy in rho_copies:
        copy.start()
    rho_in[t] = dens[t]
    own_tri.wait()
    for copy in tri_copies:
        copy.wait_recv()
    for copy in rho_copies:
        copy.wait_recv()

    contract = (((1,), (1,)), ((), ()))

    def dot(a, b):
        return lax.dot_general(a, b, contract, precision=HIGH, preferred_element_type=jnp.float32)

    gram = jnp.zeros((total, total), jnp.float32)
    for r in range(piece):
        left = tri_in[:, :, r, :].reshape(total, nz)
        right = rho_in[:, :, r, :].reshape(total, nz)
        gram = gram + dot(left, right) + dot(right, left)
    pick = (order[...] == lax.broadcasted_iota(jnp.int32, (total, total), 1)).astype(jnp.float32)
    half_way = jnp.dot(pick, gram, precision=HIGH, preferred_element_type=jnp.float32)
    factor = 1.0 / jnp.sqrt(jnp.float32(planes * ns * ny * nz * norb))
    final = dot(half_way, pick) * factor
    owned = total // (nt * ns)
    for r in range(nt * ns):
        rows_out[r] = final[r * owned : (r + 1) * owned]

    def me():
        return (t * ns + s) * nf + f

    def row_copy(k):
        pt, ps, pf = device(k)
        return remote(
            rows_out.at[pt * ns + ps], rows_in.at[me()], row_s.at[k], row_r.at[k], trial=pt, slab=ps, freq=pf
        )

    def each(action):
        if count <= 64:
            for k in range(1, count):
                action(k)
        else:
            pl.loop(1, count)(action)

    each(lambda k: row_copy(k).start())
    rows_in[me()] = rows_out[t * ns + s]
    each(lambda k: row_copy(k).wait())
    out[...] = jnp.sum(rows_in[...], axis=0)

    for copy in orb_copies + pass_copies + par_copies + tri_copies + rho_copies:
        copy.wait_send()

    @pl.when(s > 0)
    def _():
        for copy in down:
            copy.wait_send()

    @pl.when(s < ns - 1)
    def _():
        up.wait_send()


def local(sizes, orbitals, energies, potential, trials, cheb, shifts, column_order):
    nt, ns, nf = sizes
    per, planes, ny, nz = trials.shape
    norb = orbitals.shape[0] * nt
    half = ny // nf
    full = half + 16
    total = nt * per
    piece = planes * half // nt
    owned = total // (nt * ns)
    count = nt * ns * nf
    column = jnp.concatenate([energies, cheb[0], shifts, jnp.zeros((2,), jnp.float32)])
    par = jnp.broadcast_to(column[:, None], (8, 128))
    f32 = jnp.float32
    dma = pltpu.SemaphoreType.DMA
    anywhere = pl.BlockSpec(memory_space=pl.ANY)
    vmem = pl.BlockSpec(memory_space=pltpu.VMEM)
    return pl.pallas_call(
        functools.partial(kernel, sizes),
        out_shape=jax.ShapeDtypeStruct((owned, total), f32),
        in_specs=[anywhere, vmem, anywhere, anywhere, vmem],
        out_specs=vmem,
        scratch_shapes=[
            pltpu.VMEM((norb, planes + REACH, full, nz), f32),
            pltpu.VMEM((per, planes + REACH, full, nz), f32),
            pltpu.VMEM((planes + REACH + 1, full, nz), f32),
            pltpu.VMEM((nt, 8, 128), f32),
            pltpu.VMEM((nf, 8, 128), f32),
            pltpu.VMEM((4, norb, half, nz), f32),
            pltpu.VMEM((4, norb, 8, nz), f32),
            pltpu.VMEM((len(OFFSETS), half, nz), f32),
            pltpu.VMEM((nt, per, piece, nz), f32),
            pltpu.VMEM((nt, per, piece, nz), f32),
            pltpu.VMEM((nt, per, piece, nz), f32),
            pltpu.VMEM((nt * ns, owned, total), f32),
            pltpu.VMEM((count, owned, total), f32),
            dma((4,)), dma((4,)), dma((nt,)), dma((nt,)), dma((nt,)), dma((nt,)), dma((nt,)), dma((nt,)),
            dma((nf,)), dma((nf,)), dma((nt,)), dma((nt,)), dma((nt,)), dma((nt,)), dma((count,)), dma((count,)),
            dma((6,)),
        ],
        compiler_params=pltpu.CompilerParams(
            collective_id=0, has_side_effects=True, vmem_limit_bytes=48 * 1024 * 1024
        ),
    )(orbitals, par, potential, trials, column_order[:, None])


def solution(mesh):
    sizes = tuple(mesh.shape[name] for name in ("trial", "slab", "freq"))
    in_specs = (
        P("trial", "slab", None, None),
        P("trial"),
        P("slab", None, None),
        P("trial", "slab", None, None),
        P("freq", None),
        P("freq"),
        P(),
    )
    out_specs = P(("trial", "slab"), None)
    return jax.shard_map(
        functools.partial(local, sizes), mesh=mesh, in_specs=in_specs, out_specs=out_specs, check_vma=False
    )
```

time: 378 us -> 62 us (0.16)
  other arithmetic: 154 us -> 0.08 us
  blocking collectives: 95.7 us -> 0 us
  Pallas kernels: 0 us -> 55.4 us
  waiting for transfers between devices: 52.1 us -> 0 us
  local copies, waits for them, and re-layouts: 42.3 us -> 5 us
  starting transfers between devices: 14.7 us -> 0 us
  between operations: 14.9 us -> 1.33 us
    unnamed x2 -> x0, blocking collectives: 90.2 us -> none
    mul x40 -> x0, other arithmetic: 86.2 us -> none  [the longest x32 70.2 us: operate(): return (coef[None] * field - 0.5 * beside) / 4.5 * keep[None]]
    pallas_call x0 -> x1, Pallas kernels: none -> 55.4 us  [local(): pl.pallas_call(functools.partial(kernel, sizes), out_shape=jax.ShapeDtype...]
    add x8 -> x0, other arithmetic: 53.4 us -> none  [per_orbital(): return (total + orbital[None, KSTEPS:KSTEPS + planes] * response, None)]
    all_gather x1 -> x0, waiting for transfers between devices: 26.7 us -> none  [local(): lax.all_gather(orbitals, 'trial', axis=0, tiled=True)]
    all_to_all x2 -> x0, waiting for transfers between devices: 22.6 us -> none  [the longest x1 22.6 us: local(): lax.all_to_all(density, 'trial', split_axis=2, concat_axis=0, tiled=True)]
    mul x16 -> x0, local copies, waits for them, and re-layouts: 15.3 us -> none  [the longest x8 7.96 us: per_orbital(): start = orbital[None] * trial_wide]
    slice x18 -> x0, local copies, waits for them, and re-layouts: 11 us -> none  [the longest x8 5.38 us: expand(): response = coeffs[0] * start + coeffs[1] * now]
  transfers between devices with their start and end apart: 5 -> 0, of which waited for: 3 -> 0; matrix products, arithmetic and copies ran while one was open for 51% -> 0% of each run, Pallas kernels for 0% -> 0%
where the time goes in v1:
time: 62 us; the launch traced here: 61.8 us
  Pallas kernels  55.4 us (89%)
  local copies, waits for them, and re-layouts  5 us (8%)
  between operations  1.33 us (2%)
    pallas_call x1, Pallas kernels, local(): pl.pallas_call(functools.partial(kernel, sizes), out_shape=jax.ShapeDtype...  55.4 us
    unnamed x11, local copies, waits for them, and re-layouts  4.84 us

profile of v1, /device:TPU:0, one launch (start us, length us, event | category | flops | bytes accessed | tf_op | source)
XLA Modules:
  0.0 61.8 jit_solution(13763216942505211009)
XLA Ops:
  1.3 0.0 copy-start.4
  1.3 0.6 %copy-done.4 = f32[1,4]{1,0:T(1,128)S(1)} copy-done((f32[1,4]{1,0:T(1,128)S(1)}, f32[1,4]{1,0:T(1,128)}, u32[]{:S(2)}) %copy-start.4) | copy-done | bytes 40
  2.0 0.1 pad_maximum_fusion
  2.0 0.0 copy-start.3
  2.0 0.1 broadcast_in_dim.4.par
  2.1 0.6 copy-done.3
  2.7 0.1 copy.8.order
  2.8 0.0 copy-start
  2.8 1.2 %copy-done = f32[8,4,64,128]{3,2,1,0:T(8,128)S(1)} copy-done((f32[8,4,64,128]{3,2,1,0:T(8,128)S(1)}, f32[8,4,64,128]{3,2,1,0:T(8,128)}, u32[]{:S(2)}) %copy-start) | copy-done | bytes 1048600
  4.0 0.0 copy-start.1
  4.0 0.9 %copy-done.1 = f32[1,4,64,128]{3,2,1,0:T(8,128)S(1)} copy-done((f32[1,4,64,128]{3,2,1,0:T(8,128)S(1)}, f32[1,4,64,128]{3,2,1,0:T(8,128)}, u32[]{:S(2)}) %copy-start.1) | copy-done | bytes 131096
  4.9 0.0 copy-start.2
  4.9 0.9 %copy-done.2 = f32[4,64,128]{2,1,0:T(8,128)S(1)} copy-done((f32[4,64,128]{2,1,0:T(8,128)S(1)}, f32[4,64,128]{2,1,0:T(8,128)}, u32[]{:S(2)}) %copy-start.2) | copy-done | bytes 131096
  5.8 55.4 %shard_map.73 = f32[4,64]{1,0:T(4,128)S(1)} custom-call(f32[1,4,64,128]{3,2,1,0:T(8,128)S(1)} %copy-done.1, f32[8,128]{1,0:T(8,128)S(1)} %broadcast_in_dim.4.par, f32[4,64,128]{2,1,0:T(8,128)S(1)} %copy-done.2, f32[8,4,64,128]{3,2,1,0:T(8,128)S(1)} %copy-done, s32[64,1]{1,0:T(8,128)S(1)} %copy.8.order), custom_call_target="tpu_custom_call" | custom-call | tf_op jit(solution)/shard_map/pallas_call | solution.py:365
  61.2 0.6 copy.12
  (1 shorter events, 0.0 us)
Async XLA Ops:
  1.3 0.7 %copy-start.4 = (f32[1,4]{1,0:T(1,128)S(1)}, f32[1,4]{1,0:T(1,128)}, u32[]{:S(2)}) copy-start(f32[1,4]{1,0:T(1,128)} %param.11) | copy-start | bytes 52
  2.0 0.7 %copy-start.3 = (s32[64]{0:T(128)S(1)}, s32[64]{0:T(128)}, u32[]{:S(2)}) copy-start(s32[64]{0:T(128)} %param.13) | copy-start | bytes 772
  2.8 1.2 %copy-start = (f32[8,4,64,128]{3,2,1,0:T(8,128)S(1)}, f32[8,4,64,128]{3,2,1,0:T(8,128)}, u32[]{:S(2)}) copy-start(f32[8,4,64,128]{3,2,1,0:T(8,128)} %tri.1) | copy-start | bytes 3145732
  4.0 0.9 %copy-start.1 = (f32[1,4,64,128]{3,2,1,0:T(8,128)S(1)}, f32[1,4,64,128]{3,2,1,0:T(8,128)}, u32[]{:S(2)}) copy-start(f32[1,4,64,128]{3,2,1,0:T(8,128)} %orb.1) | copy-start | bytes 393220
  4.9 0.9 %copy-start.2 = (f32[4,64,128]{2,1,0:T(8,128)S(1)}, f32[4,64,128]{2,1,0:T(8,128)}, u32[]{:S(2)}) copy-start(f32[4,64,128]{2,1,0:T(8,128)} %pot.1) | copy-start | bytes 393220

commit v2 on v1

--- a/solution.py
+++ b/solution.py
@@ -29,7 +29,7 @@
 def kernel(
     sizes, orb, par, pot, tri, order, out,
     orbs, wide, pots, pars, freqs, scaled, weights, coefs, dens, rho_in, tri_in, rows_out, rows_in,
-    near_s, near_r, orb_s, orb_r, pass_s, pass_r, par_s, par_r, frq_s, frq_r,
+    near_s, near_r, up_s, up_r, dn_s, dn_r, pass_s, pass_r, par_s, par_r, frq_s, frq_r,
     tri_s, tri_r, rho_s, rho_r, row_s, row_r, loc,
 ):
     nt, ns, nf = sizes
@@ -101,43 +101,61 @@
         remote(tri.at[:, :REACH, src_y, :], wide.at[:, planes:, dst_y, :], near_s.at[1], near_r.at[1], slab=below),
         remote(pot.at[:REACH, src_y, :], pots.at[planes + 1 :, dst_y, :], near_s.at[2], near_r.at[2], slab=below),
     ]
-    up = remote(pot.at[planes - 1, src_y, :], pots.at[0, dst_y, :], near_s.at[3], near_r.at[3], slab=above)
-
-    @pl.when(s > 0)
-    def _():
-        down[0].start()
-        down[2].start()
-        down[1].start()
-
-    @pl.when(s < ns - 1)
-    def _():
-        up.start()
+    lift = remote(pot.at[planes - 1, src_y, :], pots.at[0, dst_y, :], near_s.at[3], near_r.at[3], slab=above)
 
     par_copies = []
     for j in range(1, nt):
         par_copies.append(remote(par, pars.at[t], par_s.at[j], par_r.at[j], trial=lax.rem(t + j, nt)))
     for j in range(1, nf):
         par_copies.append(remote(par, freqs.at[f], frq_s.at[j], frq_r.at[j], freq=lax.rem(f + j, nf)))
+
+    chips = nt // 2
+    z = t // 2
+    after, before = lax.rem(t + 2, nt), lax.rem(t + nt - 2, nt)
+    parts = (slice(0, planes), slice(planes, planes + REACH))
+
+    def block(slot, part):
+        return orbs.at[slot, parts[part], dst_y, :]
+
+    def at(hops):
+        return lax.rem(t + 2 * hops + nt, nt)
+
+    def from_below(j, part, source=None):
+        here = block(at(1 - j), part)
+        return remote(here if source is None else source, here, up_s.at[j, part], up_r.at[j, part], trial=after)
+
+    def from_above(j, part, source=None):
+        here = block(at(j - 1), part)
+        return remote(here if source is None else source, here, dn_s.at[j, part], dn_r.at[j, part], trial=before)
+
+    def handed(hops, part, source=None):
+        here = block(at(hops), part)
+        index = hops + chips
+        return remote(here if source is None else source, here, pass_s.at[index, part], pass_r.at[index, part], trial=mate)
+
+    can_rise, can_sink = z + 1 < chips, z >= 1
+
+    def when(condition, action):
+        pl.when(condition)(action)
+
+    when(s > 0, lambda: down[0].start())
     for copy in par_copies:
         copy.start()
-
-    for copy in locals_:
-        copy.wait()
-
-    @pl.when(s < ns - 1)
+    own = orb.at[0, :, src_y, :]
+    when(can_rise, lambda: from_below(1, 0, own).start())
+    when(can_sink, lambda: from_above(1, 0, own).start())
+    handed(0, 0, own).start()
+
+    @pl.when(s > 0)
     def _():
-        down[0].wait_recv()
-
-    def block(slot):
-        return orbs.at[slot, :, dst_y, :]
-
-    chips = nt // 2
-    orb_copies = []
-    for j in range(1, chips):
-        orb_copies.append(remote(block(t), block(t), orb_s.at[j], orb_r.at[j], trial=lax.rem(t + 2 * j, nt)))
-    pass_copies = [remote(block(t), block(t), pass_s.at[0], pass_r.at[0], trial=mate)]
-    for copy in orb_copies + pass_copies:
-        copy.start()
+        down[2].start()
+        down[1].start()
+
+    when(s < ns - 1, lambda: lift.start())
+    when(s < ns - 1, lambda: down[0].wait_recv())
+    when(can_rise, lambda: from_below(1, 1).start())
+    when(can_sink, lambda: from_above(1, 1).start())
+    handed(0, 1).start()
 
     tri_copies = []
     span = half // piece
@@ -146,18 +164,32 @@
         y0 = pl.multiple_of(f * half + lax.rem(peer, span) * piece, 8)
         part = tri.at[:, peer // span, pl.ds(y0, piece), :]
         tri_copies.append(remote(part, tri_in.at[t], tri_s.at[j], tri_r.at[j], trial=peer))
-    for copy in tri_copies:
-        copy.start()
     y0 = pl.multiple_of(f * half + lax.rem(t, span) * piece, 8)
     own_tri = pltpu.make_async_copy(tri.at[:, t // span, pl.ds(y0, piece), :], tri_in.at[t], loc.at[5])
     own_tri.start()
 
     for j in range(1, chips):
-        orb_copies[j - 1].wait_recv()
-        source = lax.rem(t - 2 * j + nt, nt)
-        copy = remote(block(source), block(source), pass_s.at[j], pass_r.at[j], trial=mate)
-        copy.start()
-        pass_copies.append(copy)
+        if j == chips - 1:
+            for copy in tri_copies:
+                copy.start()
+        for part in range(2):
+
+            @pl.when(z >= j)
+            def _():
+                from_below(j, part).wait_recv()
+                if j + 1 < chips:
+                    when(can_rise, lambda: from_below(j + 1, part).start())
+                handed(-j, part).start()
+
+            @pl.when(z + j < chips)
+            def _():
+                from_above(j, part).wait_recv()
+                if j + 1 < chips:
+                    when(can_sink, lambda: from_above(j + 1, part).start())
+                handed(j, part).start()
+
+    for copy in locals_:
+        copy.wait()
     for copy in par_copies:
         copy.wait_recv()
 
@@ -177,17 +209,13 @@
         for n in range(4):
             weights[n, i] = jnp.broadcast_to(terms[n], weights.shape[2:])
 
-    @pl.when(s < ns - 1)
-    def _():
-        down[1].wait_recv()
-        down[2].wait_recv()
-
-    @pl.when(s > 0)
-    def _():
-        up.wait_recv()
-
-    for copy in pass_copies:
-        copy.wait_recv()
+    when(s < ns - 1, lambda: down[2].wait_recv())
+    when(s > 0, lambda: lift.wait_recv())
+    for part in range(2):
+        handed(0, part).wait_recv()
+        for j in range(1, chips):
+            when(z >= j, lambda: handed(-j, part).wait_recv())
+            when(z + j < chips, lambda: handed(j, part).wait_recv())
 
     mid = slice(8, 8 + half)
     lane = lax.broadcasted_iota(jnp.int32, (half, nz), 1)
@@ -240,15 +268,15 @@
                         coef = hop**2 * (2.0 * sums[2] + (2.0 * (here + end) + middle) * sums[3])
                 elif steps == 1:
                     here, end = local(0, 0, 0), local(dx, dy, dz)
-                    at = (column, row, depth)
+                    place = (column, row, depth)
                     size = (planes * ns, ny, nz)
                     move = (dx, dy, dz)
                     side, along = 0.0, 0.0
                     for axis in range(3):
                         if move[axis]:
-                            along = links(at[axis], size[axis]) + links(at[axis] + move[axis], size[axis])
+                            along = links(place[axis], size[axis]) + links(place[axis] + move[axis], size[axis])
                         else:
-                            side = side + links(at[axis], size[axis])
+                            side = side + links(place[axis], size[axis])
                     walks = along + 3.0 * side - 1.0
                     cubic = here * here + here * end + end * end + hop**2 * walks
                     coef = hop * (sums[1] + (here + end) * sums[2] + cubic * sums[3])
@@ -261,7 +289,25 @@
                     square = here * here + hop**2 * degree
                     cube = here * (here * here + 2.0 * hop**2 * degree) + hop**2 * near
                     coef = 0.5 * (sums[0] + here * sums[1] + square * sums[2] + cube * sums[3])
-                coefs[index] = coef
+                coefs[x, index] = coef
+        return carry
+
+    lax.fori_loop(0, planes, one_plane, 0)
+    when(s < ns - 1, lambda: down[1].wait_recv())
+
+    def rho_copy(peer):
+        return remote(dens.at[peer], rho_in.at[t], rho_s.at[peer], rho_r.at[t], trial=peer)
+
+    def send(x):
+        for h in range(span):
+            peer = x * span + h
+            when(peer != t, lambda: rho_copy(peer).start())
+
+    def plane_at(step):
+        return lax.rem(t // span + 1 + step, planes)
+
+    def densities(step, carry):
+        x = plane_at(step)
 
         def one_trial(k, carry):
             density = 0.0
@@ -271,28 +317,26 @@
                     continue
                 part = 0.0
                 for index, (dx, dy, _) in group:
-                    part = part + coefs[index] * wide[k, x + dx, 8 + dy : 8 + dy + half, :]
+                    part = part + coefs[x, index] * wide[k, x + dx, 8 + dy : 8 + dy + half, :]
                 density = density + rolled(part, -dz)
             for h in range(span):
                 dens[x * span + h, k] = density[h * piece : (h + 1) * piece]
             return carry
 
-        return lax.fori_loop(0, per, one_trial, carry)
-
-    lax.fori_loop(0, planes, one_plane, 0)
-
-    rho_copies = []
-    for j in range(1, nt):
-        peer = lax.rem(t + j, nt)
-        rho_copies.append(remote(dens.at[peer], rho_in.at[t], rho_s.at[j], rho_r.at[j], trial=peer))
-    for copy in rho_copies:
-        copy.start()
+        lax.fori_loop(0, per, one_trial, 0)
+        when(step > 0, lambda: send(plane_at(step - 1)))
+        return carry
+
+    lax.fori_loop(0, planes, densities, 0)
+    send(plane_at(planes - 1))
+
     rho_in[t] = dens[t]
     own_tri.wait()
     for copy in tri_copies:
         copy.wait_recv()
-    for copy in rho_copies:
-        copy.wait_recv()
+    for j in range(1, nt):
+        source = lax.rem(t + j, nt)
+        remote(dens.at[source], rho_in.at[source], rho_s.at[source], rho_r.at[source], trial=source).wait_recv()
 
     contract = (((1,), (1,)), ((), ()))
 
@@ -333,17 +377,28 @@
     each(lambda k: row_copy(k).wait())
     out[...] = jnp.sum(rows_in[...], axis=0)
 
-    for copy in orb_copies + pass_copies + par_copies + tri_copies + rho_copies:
+    for j in range(1, nt):
+        rho_copy(lax.rem(t + j, nt)).wait_send()
+    for copy in par_copies + tri_copies:
         copy.wait_send()
+    for part in range(2):
+        first = own if part == 0 else None
+        when(can_rise, lambda: from_below(1, part, first).wait_send())
+        when(can_sink, lambda: from_above(1, part, first).wait_send())
+        handed(0, part, first).wait_send()
+        for j in range(1, chips):
+            if j + 1 < chips:
+                when(can_rise & (z >= j), lambda: from_below(j + 1, part).wait_send())
+                when(can_sink & (z + j < chips), lambda: from_above(j + 1, part).wait_send())
+            when(z >= j, lambda: handed(-j, part).wait_send())
+            when(z + j < chips, lambda: handed(j, part).wait_send())
 
     @pl.when(s > 0)
     def _():
         for copy in down:
             copy.wait_send()
 
-    @pl.when(s < ns - 1)
-    def _():
-        up.wait_send()
+    when(s < ns - 1, lambda: lift.wait_send())
 
 
 def local(sizes, orbitals, energies, potential, trials, cheb, shifts, column_order):
@@ -356,11 +411,12 @@
     piece = planes * half // nt
     owned = total // (nt * ns)
     count = nt * ns * nf
+    chips = nt // 2
     column = jnp.concatenate([energies, cheb[0], shifts, jnp.zeros((2,), jnp.float32)])
     par = jnp.broadcast_to(column[:, None], (8, 128))
     f32 = jnp.float32
     dma = pltpu.SemaphoreType.DMA
-    anywhere = pl.BlockSpec(memory_space=pl.ANY)
+    anywhere = pl.BlockSpec(memory_space=pltpu.HBM)
     vmem = pl.BlockSpec(memory_space=pltpu.VMEM)
     return pl.pallas_call(
         functools.partial(kernel, sizes),
@@ -375,14 +431,14 @@
             pltpu.VMEM((nf, 8, 128), f32),
             pltpu.VMEM((4, norb, half, nz), f32),
             pltpu.VMEM((4, norb, 8, nz), f32),
-            pltpu.VMEM((len(OFFSETS), half, nz), f32),
+            pltpu.VMEM((planes, len(OFFSETS), half, nz), f32),
             pltpu.VMEM((nt, per, piece, nz), f32),
             pltpu.VMEM((nt, per, piece, nz), f32),
             pltpu.VMEM((nt, per, piece, nz), f32),
             pltpu.VMEM((nt * ns, owned, total), f32),
             pltpu.VMEM((count, owned, total), f32),
-            dma((4,)), dma((4,)), dma((nt,)), dma((nt,)), dma((nt,)), dma((nt,)), dma((nt,)), dma((nt,)),
-            dma((nf,)), dma((nf,)), dma((nt,)), dma((nt,)), dma((nt,)), dma((nt,)), dma((count,)), dma((count,)),
+            dma((4,)), dma((4,)), dma((chips, 2)), dma((chips, 2)), dma((chips, 2)), dma((chips, 2)),
+            dma((2 * chips, 2)), dma((2 * chips, 2)), dma((nt,)), dma((nt,)), dma((nf,)), dma((nf,)), dma((nt,)), dma((nt,)), dma((nt,)), dma((nt,)), dma((count,)), dma((count,)),
             dma((6,)),
         ],
         compiler_params=pltpu.CompilerParams(

time: 62 us -> 57.4 us (0.926)
  Pallas kernels: 55.4 us -> 50.7 us
    pallas_call x1, Pallas kernels: 55.4 us -> 50.7 us  [local(): pl.pallas_call(functools.partial(kernel, sizes), out_shape=jax.ShapeDtype...]
where the time goes in v2:
time: 57.4 us; the launch traced here: 57.1 us
  Pallas kernels  50.7 us (88%)
  local copies, waits for them, and re-layouts  5 us (9%)
  between operations  1.33 us (2%)
    pallas_call x1, Pallas kernels, local(): pl.pallas_call(functools.partial(kernel, sizes), out_shape=jax.ShapeDtype...  50.7 us
    unnamed x11, local copies, waits for them, and re-layouts  4.84 us

profile of v2, /device:TPU:0, one launch (start us, length us, event | category | flops | bytes accessed | tf_op | source)
XLA Modules:
  0.0 57.1 jit_solution(17159371020311755152)
XLA Ops:
  1.3 0.0 copy-start.4
  1.3 0.6 %copy-done.4 = f32[1,4]{1,0:T(1,128)S(1)} copy-done((f32[1,4]{1,0:T(1,128)S(1)}, f32[1,4]{1,0:T(1,128)}, u32[]{:S(2)}) %copy-start.4) | copy-done | bytes 40
  2.0 0.1 pad_maximum_fusion
  2.0 0.0 copy-start.3
  2.0 0.1 broadcast_in_dim.4.par
  2.1 0.6 %copy-done.3 = s32[64]{0:T(128)S(1)} copy-done((s32[64]{0:T(128)S(1)}, s32[64]{0:T(128)}, u32[]{:S(2)}) %copy-start.3) | copy-done | bytes 280
  2.7 0.1 copy.8.order
  2.8 0.0 copy-start
  2.8 1.2 %copy-done = f32[8,4,64,128]{3,2,1,0:T(8,128)S(1)} copy-done((f32[8,4,64,128]{3,2,1,0:T(8,128)S(1)}, f32[8,4,64,128]{3,2,1,0:T(8,128)}, u32[]{:S(2)}) %copy-start) | copy-done | bytes 1048600
  4.0 0.0 copy-start.1
  4.0 0.9 %copy-done.1 = f32[1,4,64,128]{3,2,1,0:T(8,128)S(1)} copy-done((f32[1,4,64,128]{3,2,1,0:T(8,128)S(1)}, f32[1,4,64,128]{3,2,1,0:T(8,128)}, u32[]{:S(2)}) %copy-start.1) | copy-done | bytes 131096
  4.9 0.0 copy-start.2
  4.9 0.9 %copy-done.2 = f32[4,64,128]{2,1,0:T(8,128)S(1)} copy-done((f32[4,64,128]{2,1,0:T(8,128)S(1)}, f32[4,64,128]{2,1,0:T(8,128)}, u32[]{:S(2)}) %copy-start.2) | copy-done | bytes 131096
  5.8 50.7 %shard_map.73 = f32[4,64]{1,0:T(4,128)S(1)} custom-call(f32[1,4,64,128]{3,2,1,0:T(8,128)S(1)} %copy-done.1, f32[8,128]{1,0:T(8,128)S(1)} %broadcast_in_dim.4.par, f32[4,64,128]{2,1,0:T(8,128)S(1)} %copy-done.2, f32[8,4,64,128]{3,2,1,0:T(8,128)S(1)} %copy-done, s32[64,1]{1,0:T(8,128)S(1)} %copy.8.order), custom_call_target="tpu_custom_call" | custom-call | tf_op jit(solution)/shard_map/pallas_call | solution.py:421
  56.6 0.6 %copy.12 = f32[4,64]{1,0:T(4,128)} copy(f32[4,64]{1,0:T(4,128)S(1)} %shard_map.73) | data formatting | bytes 2048
  (1 shorter events, 0.0 us)
Async XLA Ops:
  1.3 0.7 %copy-start.4 = (f32[1,4]{1,0:T(1,128)S(1)}, f32[1,4]{1,0:T(1,128)}, u32[]{:S(2)}) copy-start(f32[1,4]{1,0:T(1,128)} %param.11) | copy-start | bytes 52
  2.0 0.7 %copy-start.3 = (s32[64]{0:T(128)S(1)}, s32[64]{0:T(128)}, u32[]{:S(2)}) copy-start(s32[64]{0:T(128)} %param.13) | copy-start | bytes 772
  2.8 1.2 %copy-start = (f32[8,4,64,128]{3,2,1,0:T(8,128)S(1)}, f32[8,4,64,128]{3,2,1,0:T(8,128)}, u32[]{:S(2)}) copy-start(f32[8,4,64,128]{3,2,1,0:T(8,128)} %tri.1) | copy-start | bytes 3145732
  4.0 0.9 %copy-start.1 = (f32[1,4,64,128]{3,2,1,0:T(8,128)S(1)}, f32[1,4,64,128]{3,2,1,0:T(8,128)}, u32[]{:S(2)}) copy-start(f32[1,4,64,128]{3,2,1,0:T(8,128)} %orb.1) | copy-start | bytes 393220
  4.9 0.9 %copy-start.2 = (f32[4,64,128]{2,1,0:T(8,128)S(1)}, f32[4,64,128]{2,1,0:T(8,128)}, u32[]{:S(2)}) copy-start(f32[4,64,128]{2,1,0:T(8,128)} %pot.1) | copy-start | bytes 393220

commit v3 on v2

--- a/solution.py
+++ b/solution.py
@@ -30,7 +30,7 @@
     sizes, orb, par, pot, tri, order, out,
     orbs, wide, pots, pars, freqs, scaled, weights, coefs, dens, rho_in, tri_in, rows_out, rows_in,
     near_s, near_r, up_s, up_r, dn_s, dn_r, pass_s, pass_r, par_s, par_r, frq_s, frq_r,
-    tri_s, tri_r, rho_s, rho_r, row_s, row_r, loc,
+    tri_s, tri_r, rho_s, rho_r, row_s, row_r, loc, picks,
 ):
     nt, ns, nf = sizes
     per, planes, ny, nz = tri.shape
@@ -66,6 +66,7 @@
         pltpu.make_async_copy(pot.at[:, src_y, :], pots.at[1 : planes + 1, dst_y, :], loc.at[2]),
         pltpu.make_async_copy(par, pars.at[t], loc.at[3]),
         pltpu.make_async_copy(par, freqs.at[f], loc.at[4]),
+        pltpu.make_async_copy(order, picks, loc.at[6]),
     ]
     for copy in locals_:
         copy.start()
@@ -348,10 +349,12 @@
         left = tri_in[:, :, r, :].reshape(total, nz)
         right = rho_in[:, :, r, :].reshape(total, nz)
         gram = gram + dot(left, right) + dot(right, left)
-    pick = (order[...] == lax.broadcasted_iota(jnp.int32, (total, total), 1)).astype(jnp.float32)
-    half_way = jnp.dot(pick, gram, precision=HIGH, preferred_element_type=jnp.float32)
+    pick = (picks[...] == lax.broadcasted_iota(jnp.int32, (total, total), 0)).astype(jnp.float32)
+    half_way = lax.dot_general(
+        pick, gram, (((0,), (0,)), ((), ())), precision=HIGH, preferred_element_type=jnp.float32
+    )
     factor = 1.0 / jnp.sqrt(jnp.float32(planes * ns * ny * nz * norb))
-    final = dot(half_way, pick) * factor
+    final = jnp.dot(half_way, pick, precision=HIGH, preferred_element_type=jnp.float32) * factor
     owned = total // (nt * ns)
     for r in range(nt * ns):
         rows_out[r] = final[r * owned : (r + 1) * owned]
@@ -421,7 +424,7 @@
     return pl.pallas_call(
         functools.partial(kernel, sizes),
         out_shape=jax.ShapeDtypeStruct((owned, total), f32),
-        in_specs=[anywhere, vmem, anywhere, anywhere, vmem],
+        in_specs=[anywhere, vmem, anywhere, anywhere, anywhere],
         out_specs=vmem,
         scratch_shapes=[
             pltpu.VMEM((norb, planes + REACH, full, nz), f32),
@@ -439,12 +442,13 @@
             pltpu.VMEM((count, owned, total), f32),
             dma((4,)), dma((4,)), dma((chips, 2)), dma((chips, 2)), dma((chips, 2)), dma((chips, 2)),
             dma((2 * chips, 2)), dma((2 * chips, 2)), dma((nt,)), dma((nt,)), dma((nf,)), dma((nf,)), dma((nt,)), dma((nt,)), dma((nt,)), dma((nt,)), dma((count,)), dma((count,)),
-            dma((6,)),
+            dma((7,)),
+            pltpu.VMEM((1, total), jnp.int32),
         ],
         compiler_params=pltpu.CompilerParams(
-            collective_id=0, has_side_effects=True, vmem_limit_bytes=48 * 1024 * 1024
+            collective_id=0, has_side_effects=True, vmem_limit_bytes=67043328 - 65536
         ),
-    )(orbitals, par, potential, trials, column_order[:, None])
+    )(orbitals, par, potential, trials, column_order[None])
 
 
 def solution(mesh):

time: 57.4 us -> 55.3 us (0.963)
  local copies, waits for them, and re-layouts: 5 us -> 2.53 us
    unnamed x11 -> x3, local copies, waits for them, and re-layouts: 4.84 us -> 1.87 us
    broadcast_in_dim x1, local copies, waits for them, and re-layouts: 0.07 us -> 0.66 us  [local(): par = jnp.broadcast_to(column[:, None], (8, 128))]
where the time goes in v3:
time: 55.3 us; the launch traced here: 55 us
  Pallas kernels  51.1 us (92%)
  local copies, waits for them, and re-layouts  2.53 us (5%)
  between operations  1.32 us (2%)
    pallas_call x1, Pallas kernels, local(): pl.pallas_call(functools.partial(kernel, sizes), out_shape=jax.ShapeDtype...  51.1 us
    unnamed x3, local copies, waits for them, and re-layouts  1.87 us

profile of v3, /device:TPU:0, one launch (start us, length us, event | category | flops | bytes accessed | tf_op | source)
XLA Modules:
  0.0 55.0 jit_solution(8716257704354555864)
XLA Ops:
  1.3 0.0 copy-start
  1.3 0.6 %copy-done = f32[1,4]{1,0:T(1,128)S(1)} copy-done((f32[1,4]{1,0:T(1,128)S(1)}, f32[1,4]{1,0:T(1,128)}, u32[]{:S(2)}) %copy-start) | copy-done | bytes 40
  2.0 0.1 pad_maximum_fusion
  2.0 0.7 %broadcast_in_dim.4.par = f32[8,128]{1,0:T(8,128)} broadcast(f32[8]{0:T(128)S(1)} %pad_maximum_fusion), dimensions={0} | broadcast | bytes 4128 | tf_op jit(solution)/shard_map/broadcast_in_dim | solution.py:419
  2.7 51.1 %shard_map.73 = f32[4,64]{1,0:T(4,128)} custom-call(f32[1,4,64,128]{3,2,1,0:T(8,128)} %orb.1, f32[8,128]{1,0:T(8,128)} %broadcast_in_dim.4.par, f32[4,64,128]{2,1,0:T(8,128)} %pot.1, f32[8,4,64,128]{3,2,1,0:T(8,128)} %tri.1, s32[1,64]{1,0:T(1,128)} %bitcast.2), custom_call_target="tpu_custom_call" | custom-call | tf_op jit(solution)/shard_map/pallas_call | solution.py:424
  53.8 1.2 %copy.11 = f32[4,64]{1,0:T(4,128)} copy(f32[4,64]{1,0:T(4,128)} %shard_map.73) | data formatting | bytes 2048
  (1 shorter events, 0.0 us)
Async XLA Ops:
  1.3 0.7 %copy-start = (f32[1,4]{1,0:T(1,128)S(1)}, f32[1,4]{1,0:T(1,128)}, u32[]{:S(2)}) copy-start(f32[1,4]{1,0:T(1,128)} %param.11) | copy-start | bytes 52

commit v4 on v3

--- a/solution.py
+++ b/solution.py
@@ -140,12 +140,12 @@
         pl.when(condition)(action)
 
     when(s > 0, lambda: down[0].start())
-    for copy in par_copies:
-        copy.start()
     own = orb.at[0, :, src_y, :]
     when(can_rise, lambda: from_below(1, 0, own).start())
     when(can_sink, lambda: from_above(1, 0, own).start())
     handed(0, 0, own).start()
+    for copy in par_copies:
+        copy.start()
 
     @pl.when(s > 0)
     def _():

time: 55.3 us -> 54 us (0.976)
  Pallas kernels: 51.1 us -> 49.8 us
    pallas_call x1, Pallas kernels: 51.1 us -> 49.8 us  [local(): pl.pallas_call(functools.partial(kernel, sizes), out_shape=jax.ShapeDtype...]
where the time goes in v4:
time: 54 us; the launch traced here: 53.7 us
  Pallas kernels  49.8 us (92%)
  local copies, waits for them, and re-layouts  2.53 us (5%)
  between operations  1.32 us (2%)
    pallas_call x1, Pallas kernels, local(): pl.pallas_call(functools.partial(kernel, sizes), out_shape=jax.ShapeDtype...  49.8 us
    unnamed x3, local copies, waits for them, and re-layouts  1.87 us

profile of v4, /device:TPU:0, one launch (start us, length us, event | category | flops | bytes accessed | tf_op | source)
XLA Modules:
  0.0 53.7 jit_solution(13106240263187482370)
XLA Ops:
  1.3 0.0 copy-start
  1.3 0.6 %copy-done = f32[1,4]{1,0:T(1,128)S(1)} copy-done((f32[1,4]{1,0:T(1,128)S(1)}, f32[1,4]{1,0:T(1,128)}, u32[]{:S(2)}) %copy-start) | copy-done | bytes 40
  2.0 0.1 pad_maximum_fusion
  2.0 0.7 %broadcast_in_dim.4.par = f32[8,128]{1,0:T(8,128)} broadcast(f32[8]{0:T(128)S(1)} %pad_maximum_fusion), dimensions={0} | broadcast | bytes 4128 | tf_op jit(solution)/shard_map/broadcast_in_dim | solution.py:419
  2.7 49.8 %shard_map.73 = f32[4,64]{1,0:T(4,128)} custom-call(f32[1,4,64,128]{3,2,1,0:T(8,128)} %orb.1, f32[8,128]{1,0:T(8,128)} %broadcast_in_dim.4.par, f32[4,64,128]{2,1,0:T(8,128)} %pot.1, f32[8,4,64,128]{3,2,1,0:T(8,128)} %tri.1, s32[1,64]{1,0:T(1,128)} %bitcast.2), custom_call_target="tpu_custom_call" | custom-call | tf_op jit(solution)/shard_map/pallas_call | solution.py:424
  52.5 1.2 %copy.11 = f32[4,64]{1,0:T(4,128)} copy(f32[4,64]{1,0:T(4,128)} %shard_map.73) | data formatting | bytes 2048
  (1 shorter events, 0.0 us)
Async XLA Ops:
  1.3 0.7 %copy-start = (f32[1,4]{1,0:T(1,128)S(1)}, f32[1,4]{1,0:T(1,128)}, u32[]{:S(2)}) copy-start(f32[1,4]{1,0:T(1,128)} %param.11) | copy-start | bytes 52
